TPU v7x, 128 devices: a whole 4x4x4 slice. The times are simulated.
128 devices in a mesh: dp: 16 (over x, y), expert: 8 (over z, core).
Axes of the slice: x: 4, y: 4, z: 4, core: 2. Of those that a mesh axis runs over, the one named last changes fastest.
Arguments:
- context: bfloat16 [8192, 4096], P('dp'), may hold values from -6 to 6
- out_weight: bfloat16 [4096, 4096], P('dp', 'expert'), may hold values from -0.09375 to 0.09375
- residual: bfloat16 [8192, 4096], P('dp', 'expert'), may hold values from -6 to 6
- gate_weight: bfloat16 [8, 4096, 8192], P('expert', None, 'dp'), may hold values from -0.09375 to 0.09375
- up_weight: bfloat16 [8, 4096, 8192], P('expert', None, 'dp'), may hold values from -0.09375 to 0.09375
- down_weight: bfloat16 [8, 8192, 4096], P('expert', 'dp'), may hold values from -0.0625 to 0.0625
- gate_values: float32 [8, 512], P('expert'), may hold values from 0.2 to 1
- chosen_blocks: int32 [8, 4], replicated, may hold values from 0 to 63, as said below
- block_counts: int32 [8], replicated, may hold values from 1 to 4, as said below
Outputs:
- mixed: bfloat16 [8192, 4096], P('dp', 'expert')
Inputs may be any that keep to these rules, and one draw needn't show every extreme that they name: `chosen_blocks`: within one expert the 4 block numbers are distinct; slots from block_counts on are unused but hold valid block numbers. `block_counts`: some expert uses all 4 slots.
All inputs are finite; a program needn't handle non-finite values.
Results may differ from a plain program's by a relative error of at most 0.008.
Values may be sent and summed in bfloat16 or wider, within the bound.
A program may use at most 128 MiB of HBM per device.

v0:
```python
import jax
import jax.numpy as jnp
from jax import lax
from jax.sharding import PartitionSpec as P

BLK = 128
CAP = 4


def body(
    context,
    out_weight,
    residual,
    gate_weight,
    up_weight,
    down_weight,
    gate_values,
    chosen_blocks,
    block_counts,
):
    n_dp = lax.axis_size("dp")
    n_expert = lax.axis_size("expert")
    local_tokens = context.shape[0]
    local_width = residual.shape[1]
    model_width = context.shape[1]
    local_blocks = local_tokens // BLK
    n_blocks = local_blocks * n_dp
    piece = BLK // n_dp
    my_expert = lax.axis_index("expert")
    projected = jnp.dot(
        context,
        lax.all_gather(out_weight, "dp", axis=0, tiled=True),
        preferred_element_type=jnp.float32,
    )
    attended = (residual.astype(jnp.float32) + projected).astype(jnp.bfloat16)
    split = attended.reshape(local_blocks, n_dp, piece, local_width).transpose(1, 0, 2, 3)
    pieces = lax.all_to_all(split, "dp", 0, 0, tiled=True)
    pieces = pieces.reshape(n_blocks, piece, local_width)
    slots = jnp.take(pieces, chosen_blocks.reshape(-1), axis=0)
    slots = slots.reshape(n_expert, CAP, piece, local_width)
    mine = lax.all_to_all(slots, "expert", 0, 3, tiled=True)
    mine = mine.reshape(CAP * piece, model_width)
    picked = lax.all_gather(mine, "dp", axis=0, tiled=True)
    w_gate = gate_weight[0]
    w_up = up_weight[0]
    w_down = down_weight[0]
    gate_row = gate_values[0]
    my_count = lax.dynamic_index_in_dim(block_counts, my_expert, 0, keepdims=False)
    live = jnp.arange(CAP * BLK) // BLK < my_count
    scale = jnp.where(live, gate_row, jnp.zeros_like(gate_row))
    scale = scale.reshape(CAP, n_dp, piece).transpose(1, 0, 2).reshape(-1)
    gate = jnp.dot(picked, w_gate, preferred_element_type=jnp.float32)
    upper = jnp.dot(picked, w_up, preferred_element_type=jnp.float32)
    hidden = (jax.nn.silu(gate) * upper).astype(jnp.bfloat16)
    part = jnp.dot(hidden, w_down, preferred_element_type=jnp.float32)
    part = (part * scale[:, None]).astype(jnp.bfloat16)
    summed = lax.psum_scatter(
        part.reshape(n_dp, CAP * piece, model_width), "dp", scatter_dimension=0, tiled=True
    )
    summed = summed.reshape(CAP * piece, n_expert, local_width).transpose(1, 0, 2)
    outs = lax.all_to_all(summed, "expert", 0, 0, tiled=True)
    outs = outs.reshape(n_expert * CAP, piece * local_width)
    selector = chosen_blocks.reshape(-1)[None, :] == jnp.arange(n_blocks)[:, None]
    added = jnp.dot(selector.astype(jnp.bfloat16), outs, preferred_element_type=jnp.float32)
    added = added.reshape(n_dp, local_blocks, piece, local_width)
    back = lax.all_to_all(added, "dp", 0, 0, tiled=True)
    back = back.transpose(1, 0, 2, 3).reshape(local_tokens, local_width)
    total = attended.astype(jnp.float32) + back
    return total.astype(jnp.bfloat16)


def solution(mesh):
    in_specs = (
        P("dp", None),
        P("dp", "expert"),
        P("dp", "expert"),
        P("expert", None, "dp"),
        P("expert", None, "dp"),
        P("expert", "dp", None),
        P("expert", None),
        P(),
        P(),
    )
    out_specs = P("dp", "expert")
    return jax.shard_map(body, mesh=mesh, in_specs=in_specs, out_specs=out_specs, check_vma=False)
```

profile of v0, /device:TPU:0, one launch (start us, length us, event | category | flops | bytes accessed | tf_op | source)
XLA Modules:
  0.0 281.9 jit_solution(4458407969886781237)
XLA Ops:
  6.5 0.0 all-gather.3.cloned.1.call-start
  6.5 0.7 all-gather.3.cloned.1.call-update
  7.3 0.8 copy.29
  8.0 0.1 reshape.95
  8.1 55.3 %all-gather.3.cloned.1.call-done = bf16[4096,512]{1,0:T(8,128)(2,1)} async-done(((bf16[256,512]{1,0:T(8,128)(2,1)}), bf16[4096,512]{1,0:T(8,128)(2,1)}) %all-gather.3.cloned.1.call-update) | async-done | bytes 4194320 | tf_op jit(solution)/shard_map/all_gather | solution.py:32
  63.4 5.8 %fusion.8 = bf16[512,512]{1,0:T(8,128)(2,1)S(1)} fusion(bf16[512,4096]{1,0:T(8,128)(2,1)} %param.9, bf16[4096,512]{1,0:T(8,128)(2,1)} %all-gather.3.cloned.1.call-done, bf16[512,512]{1,0:T(8,128)(2,1)} %param.11), kind=kOutput, calls=%fused_computation.9 | convolution fusion | flops 2148270080 | bytes 9437184 | tf_op jit(solution)/shard_map/dot_general | solution.py:30
  69.2 0.0 copy-start.1
  69.3 0.0 copy-start.5
  69.3 0.8 copy.49
  70.1 5.3 %all-to-all-start = ((bf16[16,4,8,512]{3,2,1,0:T(8,128)(2,1)}), bf16[16,4,8,512]{3,2,1,0:T(8,128)(2,1)S(1)}, u32[]{:S(2)}, u32[]{:S(2)}) async-start(bf16[16,4,8,512]{3,2,1,0:T(8,128)(2,1)} %bitcast.60), calls=%async_computation | async-start | bytes 1048576 | tf_op jit(solution)/shard_map/all_to_all | solution.py:37
  75.4 0.0 all-gather.5.cloned.1.call-start
  75.4 0.0 copy-done
  75.5 0.1 copy.30
  75.6 11.3 %all-to-all-done = bf16[16,4,8,512]{3,2,1,0:T(8,128)(2,1)S(1)} async-done(((bf16[16,4,8,512]{3,2,1,0:T(8,128)(2,1)}), bf16[16,4,8,512]{3,2,1,0:T(8,128)(2,1)S(1)}, u32[]{:S(2)}, u32[]{:S(2)}) %all-to-all-start) | async-done | bytes 524320 | tf_op jit(solution)/shard_map/all_to_all | solution.py:37
  86.9 0.6 gather_fusion
  87.4 0.1 broadcast_select_fusion
  87.6 11.8 %all_to_all.30 = bf16[8,4,8,512]{3,2,1,0:T(8,128)(2,1)S(1)} all-to-all(bf16[8,4,8,512]{3,2,1,0:T(8,128)(2,1)S(1)} %broadcast_select_fusion), channel_id=1, replica_groups=mesh['dp'=16,'expert'=8] {'expert'}, dimensions={0} | all-to-all | bytes 524288 | tf_op jit(solution)/shard_map/all_to_all | solution.py:41
  99.3 0.1 copy.50
  99.5 0.8 copy.41
  100.3 0.0 all-gather.5.cloned.1.call-update
  100.3 0.0 reduce-scatter.4.cloned.1.call-start
  100.3 0.6 broadcast.96
  100.9 0.0 copy-done.1
  100.9 0.7 reduce.3
  101.6 0.1 squeeze.20
  101.7 0.0 copy-done.5
  101.7 0.7 dynamic_slice.4
  102.4 0.7 select_bitcast_fusion
  103.1 0.1 mul.19
  103.2 44.6 %all-gather.5.cloned.1.call-done = bf16[512,4096]{1,0:T(8,128)(2,1)} async-done(((bf16[32,4096]{1,0:T(8,128)(2,1)}), bf16[512,4096]{1,0:T(8,128)(2,1)}) %all-gather.5.cloned.1.call-update) | async-done | bytes 4194320 | tf_op jit(solution)/shard_map/all_gather | solution.py:43
  147.8 5.9 %fusion.3 = f32[512,512]{1,0:T(8,128)S(1)} fusion(bf16[512,4096]{1,0:T(8,128)(2,1)} %all-gather.5.cloned.1.call-done, bf16[1,4096,512]{2,1,0:T(8,128)(2,1)} %param.12), kind=kOutput, calls=%fused_computation.5 | convolution fusion | flops 2147483648 | bytes 9437184 | tf_op jit(solution)/shard_map/dot_general | solution.py:52
  153.7 0.0 copy-done.2
  153.8 0.0 copy-start.3
  153.8 2.4 fusion.9
  156.2 4.3 %multiply_convert_fusion = bf16[512,4096]{1,0:T(8,128)(2,1)} fusion(bf16[512,512]{1,0:T(8,128)(2,1)S(1)} %fusion.9, bf16[1,512,4096]{2,1,0:T(8,128)(2,1)S(1)} %copy-done.3, f32[512]{0:T(512)S(1)} %mul.19), kind=kOutput, calls=%fused_computation.1 | convolution fusion | flops 2151677952 | bytes 8914944 | tf_op jit(solution)/shard_map/dot_general | solution.py:55
  160.5 0.0 reduce-scatter.4.cloned.1.call-update
  160.6 77.4 %reduce-scatter.4.cloned.1.call-done = bf16[1,32,4096]{2,1,0:T(8,128)(2,1)} async-done(((bf16[16,32,4096]{2,1,0:T(8,128)(2,1)}), bf16[1,32,4096]{2,1,0:T(8,128)(2,1)}) %reduce-scatter.4.cloned.1.call-update) | async-done | bytes 262160
  237.9 1.0 copy.42
  239.0 0.8 copy.35
  239.7 4.4 %all-to-all-start.2 = ((bf16[8,32,512]{2,1,0:T(8,128)(2,1)}), bf16[8,32,512]{2,1,0:T(8,128)(2,1)S(1)}, u32[]{:S(2)}, u32[]{:S(2)}) async-start(bf16[8,32,512]{2,1,0:T(8,128)(2,1)} %copy.35), calls=%async_computation.2 | async-start | bytes 524288 | tf_op jit(solution)/shard_map/all_to_all | solution.py:61
  244.1 0.1 eq.26
  244.2 7.5 %all-to-all-done.2 = bf16[8,32,512]{2,1,0:T(8,128)(2,1)S(1)} async-done(((bf16[8,32,512]{2,1,0:T(8,128)(2,1)}), bf16[8,32,512]{2,1,0:T(8,128)(2,1)S(1)}, u32[]{:S(2)}, u32[]{:S(2)}) %all-to-all-start.2) | async-done | bytes 262176 | tf_op jit(solution)/shard_map/all_to_all | solution.py:61
  251.7 0.1 reshape.99
  251.8 0.3 fusion.13
  252.1 0.6 copy.37
  252.8 21.5 %all_to_all.31 = f32[16,4,8,512]{3,2,1,0:T(8,128)S(1)} all-to-all(f32[16,4,8,512]{3,2,1,0:T(8,128)S(1)} %copy.37), channel_id=1, replica_groups=mesh['dp'=16,'expert'=8] {'dp'}, dimensions={0} | all-to-all | bytes 2097152 | tf_op jit(solution)/shard_map/all_to_all | solution.py:66
  274.3 0.1 copy.38
  274.3 1.0 fusion.12
  (10 shorter events, 0.0 us)
Async XLA Ops:
  6.5 56.9 %all-gather.3.cloned.1.call-start = ((), (), s32[]{:S(2)}) async-start(), calls=%async_computation.5 | async-start | bytes 4456448 | tf_op jit(solution)/shard_map/all_gather | solution.py:32
  8.1 67.3 %copy-start = (s32[8,4]{0,1:T(4,128)S(1)}, s32[8,4]{0,1:T(4,128)}, u32[]{:S(2)}) copy-start(s32[8,4]{0,1:T(4,128)} %param.16) | copy-start | bytes 388
  69.2 31.7 %copy-start.1 = (f32[1,512]{1,0:T(1,128)S(1)}, f32[1,512]{1,0:T(1,128)}, u32[]{:S(2)}) copy-start(f32[1,512]{1,0:T(1,128)} %param.15) | copy-start | bytes 6148
  69.3 32.4 %copy-start.5 = (s32[8]{0:T(128)S(1)}, s32[8]{0:T(128)}, u32[]{:S(2)}) copy-start(s32[8]{0:T(128)} %param.17) | copy-start | bytes 100
  70.1 16.8 %all-to-all-start = ((bf16[16,4,8,512]{3,2,1,0:T(8,128)(2,1)}), bf16[16,4,8,512]{3,2,1,0:T(8,128)(2,1)S(1)}, u32[]{:S(2)}, u32[]{:S(2)}) async-start(bf16[16,4,8,512]{3,2,1,0:T(8,128)(2,1)} %bitcast.60), calls=%async_computation | async-start | bytes 1048576 | tf_op jit(solution)/shard_map/all_to_all | solution.py:37
  75.4 72.4 %all-gather.5.cloned.1.call-start = ((), (), s32[]{:S(2)}) async-start(), calls=%async_computation.6 | async-start | bytes 4456448 | tf_op jit(solution)/shard_map/all_gather | solution.py:43
  100.3 137.6 %reduce-scatter.4.cloned.1.call-start = ((), (), s32[]{:S(2)}) async-start(), calls=%async_computation.7 | async-start | bytes 4456448
  147.8 5.9 %copy-start.2 = (bf16[1,4096,512]{2,1,0:T(8,128)(2,1)S(1)}, bf16[1,4096,512]{2,1,0:T(8,128)(2,1)}, u32[]{:S(2)}) copy-start(bf16[1,4096,512]{2,1,0:T(8,128)(2,1)} %param.13) | copy-start | bytes 12582916
  147.8 5.9 %copy-start.4 = (bf16[512,4096]{1,0:T(8,128)(2,1)S(1)}, bf16[512,4096]{1,0:T(8,128)(2,1)}, u32[]{:S(2)}) copy-start(bf16[512,4096]{1,0:T(8,128)(2,1)} %all-gather.5.cloned.1.call-done) | copy-start | bytes 12582916
  153.8 2.5 copy-start.3
  239.7 11.9 %all-to-all-start.2 = ((bf16[8,32,512]{2,1,0:T(8,128)(2,1)}), bf16[8,32,512]{2,1,0:T(8,128)(2,1)S(1)}, u32[]{:S(2)}, u32[]{:S(2)}) async-start(bf16[8,32,512]{2,1,0:T(8,128)(2,1)} %copy.35), calls=%async_computation.2 | async-start | bytes 524288 | tf_op jit(solution)/shard_map/all_to_all | solution.py:61
Sparse Core Ops, SparseCore 0:
  9.5 53.8 all-gather.2
  100.4 47.3 all-gather.4
  160.7 77.1 reduce-scatter.3
where the time goes:
time: 282 us
  waiting for transfers between devices  197 us (70%)
  blocking collectives  33.3 us (12%)
  matrix products  18.9 us (7%)
  between operations  13.3 us (5%)
  starting transfers between devices  9.73 us (3%)
  local copies, waits for them, and re-layouts  7.46 us (3%)
    unnamed x4, waiting for transfers between devices  78.1 us
    all_gather x1, waiting for transfers between devices, body(): lax.all_gather(out_weight, 'dp', axis=0, tiled=True)  55.3 us
    all_gather x1, waiting for transfers between devices, body(): picked = lax.all_gather(mine, 'dp', axis=0, tiled=True)  44.6 us
    all_to_all x1, blocking collectives, body(): back = lax.all_to_all(added, 'dp', 0, 0, tiled=True)  21.5 us
    all_to_all x1, blocking collectives, body(): mine = lax.all_to_all(slots, 'expert', 0, 3, tiled=True)  11.8 us
    all_to_all x1, waiting for transfers between devices, body(): pieces = lax.all_to_all(split, 'dp', 0, 0, tiled=True)  11.3 us
    all_to_all x1, waiting for transfers between devices, body(): outs = lax.all_to_all(summed, 'expert', 0, 0, tiled=True)  7.45 us
    dot_general x1, matrix products, body(): gate = jnp.dot(picked, w_gate, preferred_element_type=jnp.float32)  5.92 us
  transfers between devices with their start and end apart: 5, of which 5 were waited for; matrix products, arithmetic and copies ran while one was open for 1% of the time, Pallas kernels for 0%

commit v1 on v0

--- a/solution.py
+++ b/solution.py
@@ -5,6 +5,27 @@
 
 BLK = 128
 CAP = 4
+
+
+def collect(x, axis, dim):
+    length, index, rows = (lax.axis_size(axis), lax.axis_index(axis), x.shape[dim])
+    right = [(i, (i + 1) % length) for i in range(length)]
+    backward = [(i, (i - 1) % length) for i in range(length)]
+    out = jnp.zeros((*x.shape[:dim], length * rows, *x.shape[dim + 1 :]), x.dtype)
+    out = lax.dynamic_update_slice_in_dim(out, x, index * rows, axis=dim)
+    from_left = from_right = x
+    half = length // 2
+    for step in range(1, half + 1):
+        from_left = lax.ppermute(from_left, axis, right)
+        out = lax.dynamic_update_slice_in_dim(
+            out, from_left, (index - step) % length * rows, axis=dim
+        )
+        if step < length - half:
+            from_right = lax.ppermute(from_right, axis, backward)
+            out = lax.dynamic_update_slice_in_dim(
+                out, from_right, (index + step) % length * rows, axis=dim
+            )
+    return out
 
 
 def body(
@@ -27,11 +48,7 @@
     n_blocks = local_blocks * n_dp
     piece = BLK // n_dp
     my_expert = lax.axis_index("expert")
-    projected = jnp.dot(
-        context,
-        lax.all_gather(out_weight, "dp", axis=0, tiled=True),
-        preferred_element_type=jnp.float32,
-    )
+    projected = jnp.dot(context, collect(out_weight, "dp", 0), preferred_element_type=jnp.float32)
     attended = (residual.astype(jnp.float32) + projected).astype(jnp.bfloat16)
     split = attended.reshape(local_blocks, n_dp, piece, local_width).transpose(1, 0, 2, 3)
     pieces = lax.all_to_all(split, "dp", 0, 0, tiled=True)

time: 282 us -> 305 us (1.082)
  starting transfers between devices: 9.73 us -> 47 us
  waiting for transfers between devices: 197 us -> 169 us
  local copies, waits for them, and re-layouts: 7.46 us -> 20.6 us
    all_gather x1 -> x0, waiting for transfers between devices: 55.3 us -> none  [body(): lax.all_gather(out_weight, 'dp', axis=0, tiled=True)]
    ppermute x0 -> x15, starting transfers between devices: none -> 38.8 us  [the longest x7 37.1 us: collect(): from_right = lax.ppermute(from_right, axis, backward)]
    ppermute x0 -> x15, waiting for transfers between devices: none -> 29.8 us  [the longest x8 22.9 us: collect(): from_left = lax.ppermute(from_left, axis, right)]
    dynamic_update_slice x0 -> x16, local copies, waits for them, and re-layouts: none -> 11.6 us  [the longest x8 5.81 us: collect(): lax.dynamic_update_slice_in_dim(out, from_left, (index - step) % length *...]
    unnamed x4 -> x3, waiting for transfers between devices: 78.1 us -> 77.5 us
  transfers between devices with their start and end apart: 5 -> 19, of which waited for: 5 -> 13; matrix products, arithmetic and copies ran while one was open for 1% -> 5% of each run, Pallas kernels for 0% -> 0%
where the time goes in v1:
time: 305 us; the launch traced here: 304 us
  waiting for transfers between devices  169 us (55%)
  starting transfers between devices  47 us (15%)
  blocking collectives  34 us (11%)
  local copies, waits for them, and re-layouts  20.6 us (7%)
  matrix products  17.6 us (6%)
  between operations  13.6 us (4%)
    unnamed x3, waiting for transfers between devices  77.5 us
    all_gather x1, waiting for transfers between devices, body(): picked = lax.all_gather(mine, 'dp', axis=0, tiled=True)  44.6 us
    ppermute x7, starting transfers between devices, collect(): from_right = lax.ppermute(from_right, axis, backward)  37.1 us
    ppermute x8, waiting for transfers between devices, collect(): from_left = lax.ppermute(from_left, axis, right)  22.9 us
    all_to_all x1, blocking collectives, body(): back = lax.all_to_all(added, 'dp', 0, 0, tiled=True)  21.5 us
    all_to_all x1, blocking collectives, body(): mine = lax.all_to_all(slots, 'expert', 0, 3, tiled=True)  12.6 us
    all_to_all x1, waiting for transfers between devices, body(): pieces = lax.all_to_all(split, 'dp', 0, 0, tiled=True)  9.88 us
    all_to_all x1, waiting for transfers between devices, body(): outs = lax.all_to_all(summed, 'expert', 0, 0, tiled=True)  7.45 us
  transfers between devices with their start and end apart: 19, of which 13 were waited for; matrix products, arithmetic and copies ran while one was open for 5% of the time, Pallas kernels for 0%

profile of v1, /device:TPU:0, one launch (start us, length us, event | category | flops | bytes accessed | tf_op | source)
XLA Modules:
  0.0 304.4 jit_solution(12259398340522167051)
XLA Ops:
  6.5 1.7 collective-permute-start
  8.2 3.7 %collective-permute-start.1 = (bf16[256,512]{1,0:T(8,128)(2,1)}, bf16[256,512]{1,0:T(8,128)(2,1)S(1)}, u32[]{:S(2)}, u32[]{:S(2)}) collective-permute-start(bf16[256,512]{1,0:T(8,128)(2,1)} %param.10), channel_id=1, source_target_pairs={{0,120},{8,0},{16,8},{24,16},{32,24},{40,32},{48,40},{56,48},{64,5... | collective-permute-start | bytes 786440 | tf_op jit(solution)/shard_map/ppermute | solution.py:24
  11.9 6.5 %collective-permute-done = bf16[256,512]{1,0:T(8,128)(2,1)S(1)} collective-permute-done((bf16[256,512]{1,0:T(8,128)(2,1)}, bf16[256,512]{1,0:T(8,128)(2,1)S(1)}, u32[]{:S(2)}, u32[]{:S(2)}) %collective-permute-start) | collective-permute-done | bytes 262176 | tf_op jit(solution)/shard_map/ppermute | solution.py:19
  18.4 5.3 %collective-permute-start.3 = (bf16[256,512]{1,0:T(8,128)(2,1)S(1)}, bf16[256,512]{1,0:T(8,128)(2,1)S(1)}, u32[]{:S(2)}, u32[]{:S(2)}) collective-permute-start(bf16[256,512]{1,0:T(8,128)(2,1)S(1)} %collective-permute-done.1), channel_id=1, source_target_pairs={{0,120},{8,0},{16,8},{24,16},{32,24},{40,32},{48,40},{56,48},{64,5... | collective-permute-start | bytes 786440 | tf_op jit(solution)/shard_map/ppermute | solution.py:24
  23.8 5.5 %collective-permute-done.2 = bf16[256,512]{1,0:T(8,128)(2,1)S(1)} collective-permute-done((bf16[256,512]{1,0:T(8,128)(2,1)S(1)}, bf16[256,512]{1,0:T(8,128)(2,1)S(1)}, u32[]{:S(2)}, u32[]{:S(2)}) %collective-permute-start.2) | collective-permute-done | bytes 262176 | tf_op jit(solution)/shard_map/ppermute | solution.py:19
  29.2 5.3 %collective-permute-start.5 = (bf16[256,512]{1,0:T(8,128)(2,1)S(1)}, bf16[256,512]{1,0:T(8,128)(2,1)S(1)}, u32[]{:S(2)}, u32[]{:S(2)}) collective-permute-start(bf16[256,512]{1,0:T(8,128)(2,1)S(1)} %collective-permute-done.3), channel_id=1, source_target_pairs={{0,120},{8,0},{16,8},{24,16},{32,24},{40,32},{48,40},{56,48},{64,5... | collective-permute-start | bytes 786440 | tf_op jit(solution)/shard_map/ppermute | solution.py:24
  34.6 4.5 %collective-permute-done.4 = bf16[256,512]{1,0:T(8,128)(2,1)S(1)} collective-permute-done((bf16[256,512]{1,0:T(8,128)(2,1)S(1)}, bf16[256,512]{1,0:T(8,128)(2,1)S(1)}, u32[]{:S(2)}, u32[]{:S(2)}) %collective-permute-start.4) | collective-permute-done | bytes 262176 | tf_op jit(solution)/shard_map/ppermute | solution.py:19
  39.1 2.2 broadcast_in_dim.17
  41.3 0.7 constant_dynamic-update-slice_fusion.15
  42.3 0.7 constant_dynamic-update-slice_fusion.14
  43.0 5.3 %collective-permute-start.7 = (bf16[256,512]{1,0:T(8,128)(2,1)S(1)}, bf16[256,512]{1,0:T(8,128)(2,1)S(1)}, u32[]{:S(2)}, u32[]{:S(2)}) collective-permute-start(bf16[256,512]{1,0:T(8,128)(2,1)S(1)} %collective-permute-done.5), channel_id=1, source_target_pairs={{0,120},{8,0},{16,8},{24,16},{32,24},{40,32},{48,40},{56,48},{64,5... | collective-permute-start | bytes 786440 | tf_op jit(solution)/shard_map/ppermute | solution.py:24
  48.3 0.7 constant_dynamic-update-slice_fusion.13
  49.7 0.7 constant_dynamic-update-slice_fusion.11
  50.5 1.7 collective-permute-done.7
  52.2 5.8 %collective-permute-start.9 = (bf16[256,512]{1,0:T(8,128)(2,1)S(1)}, bf16[256,512]{1,0:T(8,128)(2,1)S(1)}, u32[]{:S(2)}, u32[]{:S(2)}) collective-permute-start(bf16[256,512]{1,0:T(8,128)(2,1)S(1)} %collective-permute-done.7), channel_id=1, source_target_pairs={{0,120},{8,0},{16,8},{24,16},{32,24},{40,32},{48,40},{56,48},{64,5... | collective-permute-start | bytes 786440 | tf_op jit(solution)/shard_map/ppermute | solution.py:24
  58.0 0.7 constant_dynamic-update-slice_fusion.10
  58.8 0.7 constant_dynamic-update-slice_fusion.9
  59.5 0.7 constant_dynamic-update-slice_fusion.8
  60.2 1.7 collective-permute-done.9
  61.9 5.8 %collective-permute-start.11 = (bf16[256,512]{1,0:T(8,128)(2,1)S(1)}, bf16[256,512]{1,0:T(8,128)(2,1)S(1)}, u32[]{:S(2)}, u32[]{:S(2)}) collective-permute-start(bf16[256,512]{1,0:T(8,128)(2,1)S(1)} %collective-permute-done.9), channel_id=1, source_target_pairs={{0,120},{8,0},{16,8},{24,16},{32,24},{40,32},{48,40},{56,48},{64,5... | collective-permute-start | bytes 786440 | tf_op jit(solution)/shard_map/ppermute | solution.py:24
  67.7 0.7 constant_dynamic-update-slice_fusion.7
  68.5 0.7 constant_dynamic-update-slice_fusion.6
  69.2 0.7 constant_dynamic-update-slice_fusion.5
  69.9 2.0 collective-permute-done.11
  71.9 5.8 %collective-permute-start.13 = (bf16[256,512]{1,0:T(8,128)(2,1)S(1)}, bf16[256,512]{1,0:T(8,128)(2,1)S(1)}, u32[]{:S(2)}, u32[]{:S(2)}) collective-permute-start(bf16[256,512]{1,0:T(8,128)(2,1)S(1)} %collective-permute-done.11), channel_id=1, source_target_pairs={{0,120},{8,0},{16,8},{24,16},{32,24},{40,32},{48,40},{56,48},{64,5... | collective-permute-start | bytes 786440 | tf_op jit(solution)/shard_map/ppermute | solution.py:24
  77.7 0.8 constant_dynamic-update-slice_fusion.4
  78.7 0.8 constant_dynamic-update-slice_fusion.3
  79.5 0.7 constant_dynamic-update-slice_fusion.2
  80.2 1.4 collective-permute-done.13
  82.3 6.1 %collective-permute-done.14 = bf16[256,512]{1,0:T(8,128)(2,1)S(1)} collective-permute-done((bf16[256,512]{1,0:T(8,128)(2,1)S(1)}, bf16[256,512]{1,0:T(8,128)(2,1)S(1)}, u32[]{:S(2)}, u32[]{:S(2)}) %collective-permute-start.14) | collective-permute-done | bytes 262176 | tf_op jit(solution)/shard_map/ppermute | solution.py:19
  88.4 0.7 constant_dynamic-update-slice_fusion
  89.1 4.5 %fusion.9 = bf16[512,512]{1,0:T(8,128)(2,1)S(1)} fusion(bf16[512,4096]{1,0:T(8,128)(2,1)S(1)} %copy-done.3, bf16[4096,512]{1,0:T(8,128)(2,1)} %constant_dynamic-update-slice_fusion, bf16[512,512]{1,0:T(8,128)(2,1)S(1)} %copy-done.7), kind=kOutput, calls=%fused_computation.10 | convolution fusion | flops 2148270080 | bytes 9437184 | tf_op jit(solution)/shard_map/dot_general | solution.py:51
  93.7 0.9 copy.49
  94.6 3.6 %all-to-all-start = ((bf16[16,4,8,512]{3,2,1,0:T(8,128)(2,1)}), bf16[16,4,8,512]{3,2,1,0:T(8,128)(2,1)S(1)}, u32[]{:S(2)}, u32[]{:S(2)}) async-start(bf16[16,4,8,512]{3,2,1,0:T(8,128)(2,1)} %bitcast.66), calls=%async_computation | async-start | bytes 1048576 | tf_op jit(solution)/shard_map/all_to_all | solution.py:54
  98.3 9.9 %all-to-all-done = bf16[16,4,8,512]{3,2,1,0:T(8,128)(2,1)S(1)} async-done(((bf16[16,4,8,512]{3,2,1,0:T(8,128)(2,1)}), bf16[16,4,8,512]{3,2,1,0:T(8,128)(2,1)S(1)}, u32[]{:S(2)}, u32[]{:S(2)}) %all-to-all-start) | async-done | bytes 524320 | tf_op jit(solution)/shard_map/all_to_all | solution.py:54
  108.9 12.6 %all_to_all.30 = bf16[8,4,8,512]{3,2,1,0:T(8,128)(2,1)S(1)} all-to-all(bf16[8,4,8,512]{3,2,1,0:T(8,128)(2,1)S(1)} %broadcast_select_fusion), channel_id=1, replica_groups=mesh['dp'=16,'expert'=8] {'expert'}, dimensions={0} | all-to-all | bytes 524288 | tf_op jit(solution)/shard_map/all_to_all | solution.py:58
  121.6 0.8 copy.41
  125.3 44.6 %all-gather.2.cloned.1.call-done = bf16[512,4096]{1,0:T(8,128)(2,1)} async-done(((bf16[32,4096]{1,0:T(8,128)(2,1)}), bf16[512,4096]{1,0:T(8,128)(2,1)}) %all-gather.2.cloned.1.call-update) | async-done | bytes 4194320 | tf_op jit(solution)/shard_map/all_gather | solution.py:60
  169.9 5.9 %fusion.3 = f32[512,512]{1,0:T(8,128)S(1)} fusion(bf16[512,4096]{1,0:T(8,128)(2,1)} %all-gather.2.cloned.1.call-done, bf16[1,4096,512]{2,1,0:T(8,128)(2,1)} %param.12), kind=kOutput, calls=%fused_computation.5 | convolution fusion | flops 2147483648 | bytes 9437184 | tf_op jit(solution)/shard_map/dot_general | solution.py:69
  175.9 2.4 fusion.10
  178.3 4.3 %multiply_convert_fusion = bf16[512,4096]{1,0:T(8,128)(2,1)} fusion(bf16[512,512]{1,0:T(8,128)(2,1)S(1)} %fusion.10, bf16[1,512,4096]{2,1,0:T(8,128)(2,1)S(1)} %copy-done.5, f32[512]{0:T(512)S(1)} %mul.83), kind=kOutput, calls=%fused_computation.1 | convolution fusion | flops 2151677952 | bytes 8914944 | tf_op jit(solution)/shard_map/dot_general | solution.py:72
  182.7 77.4 %reduce-scatter.4.cloned.1.call-done = bf16[1,32,4096]{2,1,0:T(8,128)(2,1)} async-done(((bf16[16,32,4096]{2,1,0:T(8,128)(2,1)}), bf16[1,32,4096]{2,1,0:T(8,128)(2,1)}) %reduce-scatter.4.cloned.1.call-update) | async-done | bytes 262160
  260.1 1.0 copy.42
  261.1 0.8 copy.35
  261.9 4.4 %all-to-all-start.2 = ((bf16[8,32,512]{2,1,0:T(8,128)(2,1)}), bf16[8,32,512]{2,1,0:T(8,128)(2,1)S(1)}, u32[]{:S(2)}, u32[]{:S(2)}) async-start(bf16[8,32,512]{2,1,0:T(8,128)(2,1)} %copy.35), calls=%async_computation.2 | async-start | bytes 524288 | tf_op jit(solution)/shard_map/all_to_all | solution.py:78
  266.5 7.5 %all-to-all-done.2 = bf16[8,32,512]{2,1,0:T(8,128)(2,1)S(1)} async-done(((bf16[8,32,512]{2,1,0:T(8,128)(2,1)}), bf16[8,32,512]{2,1,0:T(8,128)(2,1)S(1)}, u32[]{:S(2)}, u32[]{:S(2)}) %all-to-all-start.2) | async-done | bytes 262176 | tf_op jit(solution)/shard_map/all_to_all | solution.py:78
  275.0 21.5 %all_to_all.31 = f32[16,4,8,512]{3,2,1,0:T(8,128)S(1)} all-to-all(f32[16,4,8,512]{3,2,1,0:T(8,128)S(1)} %copy.37), channel_id=1, replica_groups=mesh['dp'=16,'expert'=8] {'dp'}, dimensions={0} | all-to-all | bytes 2097152 | tf_op jit(solution)/shard_map/all_to_all | solution.py:83
  296.6 1.0 fusion.13
  (60 shorter events, 7.1 us)
Async XLA Ops:
  6.5 34.8 %copy-start = (bf16[256,512]{1,0:T(8,128)(2,1)S(1)}, bf16[256,512]{1,0:T(8,128)(2,1)}, u32[]{:S(2)}) copy-start(bf16[256,512]{1,0:T(8,128)(2,1)} %param.10) | copy-start | bytes 786436
  6.5 35.5 %copy-start.1 = (s32[8,4]{0,1:T(4,128)S(1)}, s32[8,4]{0,1:T(4,128)}, u32[]{:S(2)}) copy-start(s32[8,4]{0,1:T(4,128)} %param.16) | copy-start | bytes 388
  6.5 11.9 %collective-permute-start = (bf16[256,512]{1,0:T(8,128)(2,1)}, bf16[256,512]{1,0:T(8,128)(2,1)S(1)}, u32[]{:S(2)}, u32[]{:S(2)}) collective-permute-start(bf16[256,512]{1,0:T(8,128)(2,1)} %param.10), channel_id=1, source_target_pairs={{0,8},{8,16},{16,24},{24,32},{32,40},{40,48},{48,56},{56,64},{64,7... | collective-permute-start | bytes 786440 | tf_op jit(solution)/shard_map/ppermute | solution.py:19
  8.2 10.2 %collective-permute-start.1 = (bf16[256,512]{1,0:T(8,128)(2,1)}, bf16[256,512]{1,0:T(8,128)(2,1)S(1)}, u32[]{:S(2)}, u32[]{:S(2)}) collective-permute-start(bf16[256,512]{1,0:T(8,128)(2,1)} %param.10), channel_id=1, source_target_pairs={{0,120},{8,0},{16,8},{24,16},{32,24},{40,32},{48,40},{56,48},{64,5... | collective-permute-start | bytes 786440 | tf_op jit(solution)/shard_map/ppermute | solution.py:24
  18.4 10.8 %collective-permute-start.2 = (bf16[256,512]{1,0:T(8,128)(2,1)S(1)}, bf16[256,512]{1,0:T(8,128)(2,1)S(1)}, u32[]{:S(2)}, u32[]{:S(2)}) collective-permute-start(bf16[256,512]{1,0:T(8,128)(2,1)S(1)} %collective-permute-done), channel_id=1, source_target_pairs={{0,8},{8,16},{16,24},{24,32},{32,40},{40,48},{48,56},{56,64},{64,7... | collective-permute-start | bytes 786440 | tf_op jit(solution)/shard_map/ppermute | solution.py:19
  18.4 10.8 %collective-permute-start.3 = (bf16[256,512]{1,0:T(8,128)(2,1)S(1)}, bf16[256,512]{1,0:T(8,128)(2,1)S(1)}, u32[]{:S(2)}, u32[]{:S(2)}) collective-permute-start(bf16[256,512]{1,0:T(8,128)(2,1)S(1)} %collective-permute-done.1), channel_id=1, source_target_pairs={{0,120},{8,0},{16,8},{24,16},{32,24},{40,32},{48,40},{56,48},{64,5... | collective-permute-start | bytes 786440 | tf_op jit(solution)/shard_map/ppermute | solution.py:24
  29.2 9.9 %collective-permute-start.4 = (bf16[256,512]{1,0:T(8,128)(2,1)S(1)}, bf16[256,512]{1,0:T(8,128)(2,1)S(1)}, u32[]{:S(2)}, u32[]{:S(2)}) collective-permute-start(bf16[256,512]{1,0:T(8,128)(2,1)S(1)} %collective-permute-done.2), channel_id=1, source_target_pairs={{0,8},{8,16},{16,24},{24,32},{32,40},{40,48},{48,56},{56,64},{64,7... | collective-permute-start | bytes 786440 | tf_op jit(solution)/shard_map/ppermute | solution.py:19
  29.2 13.8 %collective-permute-start.5 = (bf16[256,512]{1,0:T(8,128)(2,1)S(1)}, bf16[256,512]{1,0:T(8,128)(2,1)S(1)}, u32[]{:S(2)}, u32[]{:S(2)}) collective-permute-start(bf16[256,512]{1,0:T(8,128)(2,1)S(1)} %collective-permute-done.3), channel_id=1, source_target_pairs={{0,120},{8,0},{16,8},{24,16},{32,24},{40,32},{48,40},{56,48},{64,5... | collective-permute-start | bytes 786440 | tf_op jit(solution)/shard_map/ppermute | solution.py:24
  39.1 9.9 %collective-permute-start.6 = (bf16[256,512]{1,0:T(8,128)(2,1)S(1)}, bf16[256,512]{1,0:T(8,128)(2,1)S(1)}, u32[]{:S(2)}, u32[]{:S(2)}) collective-permute-start(bf16[256,512]{1,0:T(8,128)(2,1)S(1)} %collective-permute-done.4), channel_id=1, source_target_pairs={{0,8},{8,16},{16,24},{24,32},{32,40},{40,48},{48,56},{56,64},{64,7... | collective-permute-start | bytes 786440 | tf_op jit(solution)/shard_map/ppermute | solution.py:19
  42.1 47.1 %copy-start.7 = (bf16[512,512]{1,0:T(8,128)(2,1)S(1)}, bf16[512,512]{1,0:T(8,128)(2,1)}, u32[]{:S(2)}) copy-start(bf16[512,512]{1,0:T(8,128)(2,1)} %param.11) | copy-start | bytes 1572868
  42.3 46.9 %copy-start.3 = (bf16[512,4096]{1,0:T(8,128)(2,1)S(1)}, bf16[512,4096]{1,0:T(8,128)(2,1)}, u32[]{:S(2)}) copy-start(bf16[512,4096]{1,0:T(8,128)(2,1)} %param.9) | copy-start | bytes 12582916
  43.0 9.2 %collective-permute-start.7 = (bf16[256,512]{1,0:T(8,128)(2,1)S(1)}, bf16[256,512]{1,0:T(8,128)(2,1)S(1)}, u32[]{:S(2)}, u32[]{:S(2)}) collective-permute-start(bf16[256,512]{1,0:T(8,128)(2,1)S(1)} %collective-permute-done.5), channel_id=1, source_target_pairs={{0,120},{8,0},{16,8},{24,16},{32,24},{40,32},{48,40},{56,48},{64,5... | collective-permute-start | bytes 786440 | tf_op jit(solution)/shard_map/ppermute | solution.py:24
  49.0 9.7 %collective-permute-start.8 = (bf16[256,512]{1,0:T(8,128)(2,1)S(1)}, bf16[256,512]{1,0:T(8,128)(2,1)S(1)}, u32[]{:S(2)}, u32[]{:S(2)}) collective-permute-start(bf16[256,512]{1,0:T(8,128)(2,1)S(1)} %collective-permute-done.6), channel_id=1, source_target_pairs={{0,8},{8,16},{16,24},{24,32},{32,40},{40,48},{48,56},{56,64},{64,7... | collective-permute-start | bytes 786440 | tf_op jit(solution)/shard_map/ppermute | solution.py:19
  52.2 9.7 %collective-permute-start.9 = (bf16[256,512]{1,0:T(8,128)(2,1)S(1)}, bf16[256,512]{1,0:T(8,128)(2,1)S(1)}, u32[]{:S(2)}, u32[]{:S(2)}) collective-permute-start(bf16[256,512]{1,0:T(8,128)(2,1)S(1)} %collective-permute-done.7), channel_id=1, source_target_pairs={{0,120},{8,0},{16,8},{24,16},{32,24},{40,32},{48,40},{56,48},{64,5... | collective-permute-start | bytes 786440 | tf_op jit(solution)/shard_map/ppermute | solution.py:24
  58.8 9.7 %collective-permute-start.10 = (bf16[256,512]{1,0:T(8,128)(2,1)S(1)}, bf16[256,512]{1,0:T(8,128)(2,1)S(1)}, u32[]{:S(2)}, u32[]{:S(2)}) collective-permute-start(bf16[256,512]{1,0:T(8,128)(2,1)S(1)} %collective-permute-done.8), channel_id=1, source_target_pairs={{0,8},{8,16},{16,24},{24,32},{32,40},{40,48},{48,56},{56,64},{64,7... | collective-permute-start | bytes 786440 | tf_op jit(solution)/shard_map/ppermute | solution.py:19
  61.9 10.0 %collective-permute-start.11 = (bf16[256,512]{1,0:T(8,128)(2,1)S(1)}, bf16[256,512]{1,0:T(8,128)(2,1)S(1)}, u32[]{:S(2)}, u32[]{:S(2)}) collective-permute-start(bf16[256,512]{1,0:T(8,128)(2,1)S(1)} %collective-permute-done.9), channel_id=1, source_target_pairs={{0,120},{8,0},{16,8},{24,16},{32,24},{40,32},{48,40},{56,48},{64,5... | collective-permute-start | bytes 786440 | tf_op jit(solution)/shard_map/ppermute | solution.py:24
  68.4 10.3 %collective-permute-start.12 = (bf16[256,512]{1,0:T(8,128)(2,1)S(1)}, bf16[256,512]{1,0:T(8,128)(2,1)S(1)}, u32[]{:S(2)}, u32[]{:S(2)}) collective-permute-start(bf16[256,512]{1,0:T(8,128)(2,1)S(1)} %collective-permute-done.10), channel_id=1, source_target_pairs={{0,8},{8,16},{16,24},{24,32},{32,40},{40,48},{48,56},{56,64},{64,7... | collective-permute-start | bytes 786440 | tf_op jit(solution)/shard_map/ppermute | solution.py:19
  71.9 9.7 %collective-permute-start.13 = (bf16[256,512]{1,0:T(8,128)(2,1)S(1)}, bf16[256,512]{1,0:T(8,128)(2,1)S(1)}, u32[]{:S(2)}, u32[]{:S(2)}) collective-permute-start(bf16[256,512]{1,0:T(8,128)(2,1)S(1)} %collective-permute-done.11), channel_id=1, source_target_pairs={{0,120},{8,0},{16,8},{24,16},{32,24},{40,32},{48,40},{56,48},{64,5... | collective-permute-start | bytes 786440 | tf_op jit(solution)/shard_map/ppermute | solution.py:24
  78.7 9.7 %collective-permute-start.14 = (bf16[256,512]{1,0:T(8,128)(2,1)S(1)}, bf16[256,512]{1,0:T(8,128)(2,1)S(1)}, u32[]{:S(2)}, u32[]{:S(2)}) collective-permute-start(bf16[256,512]{1,0:T(8,128)(2,1)S(1)} %collective-permute-done.12), channel_id=1, source_target_pairs={{0,8},{8,16},{16,24},{24,32},{32,40},{40,48},{48,56},{56,64},{64,7... | collective-permute-start | bytes 786440 | tf_op jit(solution)/shard_map/ppermute | solution.py:19
  93.7 29.5 %copy-start.2 = (f32[1,512]{1,0:T(1,128)S(1)}, f32[1,512]{1,0:T(1,128)}, u32[]{:S(2)}) copy-start(f32[1,512]{1,0:T(1,128)} %param.15) | copy-start | bytes 6148
  93.7 30.2 %copy-start.8 = (s32[8]{0:T(128)S(1)}, s32[8]{0:T(128)}, u32[]{:S(2)}) copy-start(s32[8]{0:T(128)} %param.17) | copy-start | bytes 100
  94.6 13.6 %all-to-all-start = ((bf16[16,4,8,512]{3,2,1,0:T(8,128)(2,1)}), bf16[16,4,8,512]{3,2,1,0:T(8,128)(2,1)S(1)}, u32[]{:S(2)}, u32[]{:S(2)}) async-start(bf16[16,4,8,512]{3,2,1,0:T(8,128)(2,1)} %bitcast.66), calls=%async_computation | async-start | bytes 1048576 | tf_op jit(solution)/shard_map/all_to_all | solution.py:54
  98.1 71.8 %all-gather.2.cloned.1.call-start = ((), (), s32[]{:S(2)}) async-start(), calls=%async_computation.5 | async-start | bytes 4456448 | tf_op jit(solution)/shard_map/all_gather | solution.py:60
  122.4 137.7 %reduce-scatter.4.cloned.1.call-start = ((), (), s32[]{:S(2)}) async-start(), calls=%async_computation.6 | async-start | bytes 4456448
  169.9 5.9 %copy-start.4 = (bf16[1,4096,512]{2,1,0:T(8,128)(2,1)S(1)}, bf16[1,4096,512]{2,1,0:T(8,128)(2,1)}, u32[]{:S(2)}) copy-start(bf16[1,4096,512]{2,1,0:T(8,128)(2,1)} %param.13) | copy-start | bytes 12582916
  169.9 5.9 %copy-start.6 = (bf16[512,4096]{1,0:T(8,128)(2,1)S(1)}, bf16[512,4096]{1,0:T(8,128)(2,1)}, u32[]{:S(2)}) copy-start(bf16[512,4096]{1,0:T(8,128)(2,1)} %all-gather.2.cloned.1.call-done) | copy-start | bytes 12582916
  175.9 2.5 copy-start.5
  261.9 12.0 %all-to-all-start.2 = ((bf16[8,32,512]{2,1,0:T(8,128)(2,1)}), bf16[8,32,512]{2,1,0:T(8,128)(2,1)S(1)}, u32[]{:S(2)}, u32[]{:S(2)}) async-start(bf16[8,32,512]{2,1,0:T(8,128)(2,1)} %copy.35), calls=%async_computation.2 | async-start | bytes 524288 | tf_op jit(solution)/shard_map/all_to_all | solution.py:78
Sparse Core Ops, SparseCore 0:
  122.5 47.3 all-gather.1
  182.8 77.2 reduce-scatter.3
